TPU v7x, 32 devices: a whole 2x2x4 slice. The times are simulated.
32 devices in a mesh: grp: 4 (over y, x), dev: 8 (over z, core).
Axes of the slice: x: 2, y: 2, z: 4, core: 2. Of those that a mesh axis runs over, the one named last changes fastest.
Arguments:
- particles: float32 [128, 5, 128], P(('grp', 'dev')), as said below
- entropy: float32 [128, 128], P(('grp', 'dev')), may hold values from 0.5 to 2
- lists: int32 [128, 64], P(('grp', 'dev')), may hold values from 0 to 127, as said below
- counts: int32 [128], P(('grp', 'dev')), may hold values from 16 to 64, as said below
Outputs:
- density: float32 [128, 128], P(('grp', 'dev'))
- accel: float32 [128, 3, 128], P(('grp', 'dev'))
Inputs may be any that keep to these rules, and one draw needn't show every extreme that they name: lists[c, 0] = c; every id lies in the group of c or in one of the two groups next to it, counting groups of 32 cells around a loop. `counts`: each count is a multiple of 16. `particles`: coordinates in 0 to 1 within the group's slab, masses positive, smoothing lengths from 0.3 to 0.6.
All inputs are finite; a program needn't handle non-finite values.
Results may differ from a plain program's by a relative error of at most 0.0003.
Values sent between devices are 32-bit elements; how exact they have to be, the bound alone decides.
No kernel may reach another device: no remote copies, remote signals or barrier semaphores. Data moves between devices by JAX's collectives and lax.ppermute only.
A program may use at most 64 MiB of HBM per device.

v0:
```python
import math
import jax
import jax.numpy as jnp
from jax import lax
from jax.sharding import PartitionSpec as P

NB = 64
NBLK = 8
norm_const = 21.0 / (16.0 * math.pi)


def padded(block, sides, width):
    for axis, dim in sides:
        count = lax.axis_size(axis)
        forward = [(i, i + 1) for i in range(count - 1)]
        forward.append((count - 1, 0))
        backward = [(target, source) for source, target in forward]
        low = lax.ppermute(
            lax.slice_in_dim(block, block.shape[dim] - width, None, axis=dim), axis, forward
        )
        high = lax.ppermute(lax.slice_in_dim(block, 0, width, axis=dim), axis, backward)
        block = jnp.concatenate([low, block, high], axis=dim)
    return block


def kernel_parts(dist_sq, smooth):
    ratio = jnp.sqrt(dist_sq) / smooth
    base_of = jnp.maximum(1.0 - 0.5 * ratio, 0.0)
    kernel = norm_const / smooth**3 * base_of**4 * (1.0 + 2.0 * ratio)
    slope = -5.0 * norm_const / smooth**5 * base_of**3
    return (kernel, slope)


def on_device(particles, entropy, lists, counts):
    own_cells = particles.shape[0]
    groups = lax.axis_size("grp")
    members = lax.axis_size("dev")
    group_cells = own_cells * members
    group_at = lax.axis_index("grp")
    group_of = lists // group_cells
    within = lists % group_cells
    side_of = (group_of - group_at + 1 + groups) % groups
    shift_all = (side_of - 1).astype(jnp.float32)
    member_of = within // own_cells
    cell_of = within % own_cells
    rimmed = padded(particles, (("grp", 0),), own_cells)
    extended = lax.all_gather(rimmed, "dev", axis=0, tiled=True)
    slots_ext = member_of * (3 * own_cells) + side_of * own_cells + cell_of
    upper = NB // NBLK
    slot_range = jnp.arange(NBLK, dtype=jnp.int32)
    own_smooth = particles[:, None, 4, :, None]
    unit_first = jnp.array([1.0, 0.0, 0.0], dtype=jnp.float32)

    def fetch_block(block_at):
        chosen = lax.dynamic_slice_in_dim(slots_ext, block_at * NBLK, NBLK, 1)
        shift_blk = lax.dynamic_slice_in_dim(shift_all, block_at * NBLK, NBLK, 1)
        others = extended[chosen]
        live = ((block_at * NBLK + slot_range)[None, :] < counts[:, None]).astype(jnp.float32)
        offset = particles[:, None, :3, :, None] - others[:, :, :3, None, :]
        offset = offset - shift_blk[:, :, None, None, None] * unit_first[None, None, :, None, None]
        dist_sq = jnp.sum(offset * offset, axis=2)
        return (chosen, others, live, offset, dist_sq)

    def density_step(block_at, total):
        chosen, others, live, offset, dist_sq = fetch_block(block_at)
        kernel, slope = kernel_parts(dist_sq, own_smooth)
        return total + jnp.sum(
            live[:, :, None, None] * others[:, :, 3, None, :] * kernel, axis=(1, 3)
        )

    density = lax.fori_loop(
        0, upper, density_step, jnp.zeros((own_cells, particles.shape[2]), jnp.float32)
    )
    pressure = entropy * density ** (5.0 / 3.0)
    weight = pressure / (density * density)
    weight_rim = padded(weight, (("grp", 0),), own_cells)
    weight_ext = lax.all_gather(weight_rim, "dev", axis=0, tiled=True)

    def force_step(block_at, total):
        chosen, others, live, offset, dist_sq = fetch_block(block_at)
        kernel_i, slope_i = kernel_parts(dist_sq, own_smooth)
        kernel_j, slope_j = kernel_parts(dist_sq, others[:, :, 4, None, :])
        factor = (
            live[:, :, None, None]
            * others[:, :, 3, None, :]
            * (weight[:, None, :, None] * slope_i + weight_ext[chosen][:, :, None, :] * slope_j)
        )
        return total - jnp.sum(factor[:, :, None] * offset, axis=(1, 4))

    accel = lax.fori_loop(
        0, upper, force_step, jnp.zeros((own_cells, 3, particles.shape[2]), jnp.float32)
    )
    return (density, accel)


def solution(mesh):
    return jax.shard_map(
        on_device,
        mesh=mesh,
        in_specs=(
            P(("grp", "dev"), None, None),
            P(("grp", "dev"), None),
            P(("grp", "dev"), None),
            P(("grp", "dev")),
        ),
        out_specs=(P(("grp", "dev"), None), P(("grp", "dev"), None, None)),
        check_vma=False,
    )
```

profile of v0, /device:TPU:0, one launch (start us, length us, event | category | flops | bytes accessed | tf_op | source)
XLA Modules:
  0.0 148.0 jit_solution(8237750292582553730)
XLA Ops:
  1.3 3.9 %collective-permute-start.1 = (f32[4,5,128]{2,1,0:T(8,128)S(1)}, f32[4,5,128]{2,1,0:T(8,128)S(1)}, u32[]{:S(2)}, u32[]{:S(2)}) collective-permute-start(f32[4,5,128]{2,1,0:T(8,128)S(1)} %copy.28), channel_id=1, source_target_pairs={{8,0},{16,8},{24,16},{0,24},{9,1},{17,9},{25,17},{1,25},{10,2},{18... | collective-permute-start | bytes 30728 | tf_op jit(solution)/shard_map/ppermute | solution.py:21
  8.0 1.9 %collective-permute-done = f32[4,5,128]{2,1,0:T(8,128)S(1)} collective-permute-done((f32[4,5,128]{2,1,0:T(8,128)S(1)}, f32[4,5,128]{2,1,0:T(8,128)S(1)}, u32[]{:S(2)}, u32[]{:S(2)}) %collective-permute-start) | collective-permute-done | bytes 10272 | tf_op jit(solution)/shard_map/ppermute | solution.py:18
  9.9 14.7 %all_gather.6 = f32[96,5,128]{2,1,0:T(8,128)S(1)} all-gather(f32[12,5,128]{2,1,0:T(8,128)S(1)} %pad_maximum_fusion), channel_id=1, replica_groups=mesh['grp'=4,'dev'=8] {'dev'}, dimensions={0}, use_global_device_ids=true | all-gather | bytes 276480 | tf_op jit(solution)/shard_map/all_gather | solution.py:47
  24.6 41.9 %while.34 = (s32[]{:T(128)}, f32[4,128]{1,0:T(4,128)S(1)}, s32[4]{0:T(128)}, s32[4,64]{1,0:T(4,128)S(1)}, f32[96,5,128]{2,1,0:T(8,128)S(1)}, /*index=5*/f32[4,1,...) while((s32[]{:T(128)}, f32[4,128]{1,0:T(4,128)S(1)}, ...), condition=%wide.region_3.4_spmd.clone.clone, body=%wide.region_0.3_spmd.sunk.clone.clone.sunk | while | flops 12065039 | bytes 4628909 | solution.py:71
  28.4 1.4 multiply_reduce_fusion.9
  33.7 1.4 multiply_reduce_fusion.9
  38.9 1.4 multiply_reduce_fusion.9
  44.1 1.4 multiply_reduce_fusion.9
  49.4 1.4 multiply_reduce_fusion.9
  54.6 1.4 multiply_reduce_fusion.9
  59.9 1.4 multiply_reduce_fusion.9
  65.1 1.4 multiply_reduce_fusion.9
  68.7 1.6 %collective-permute-done.3 = f32[4,128]{1,0:T(4,128)S(1)} collective-permute-done((f32[4,128]{1,0:T(4,128)S(1)}, f32[4,128]{1,0:T(4,128)S(1)}, u32[]{:S(2)}, u32[]{:S(2)}) %collective-permute-start.3) | collective-permute-done | bytes 2080 | tf_op jit(solution)/shard_map/ppermute | solution.py:21
  70.2 2.0 %collective-permute-done.2 = f32[4,128]{1,0:T(4,128)S(1)} collective-permute-done((f32[4,128]{1,0:T(4,128)S(1)}, f32[4,128]{1,0:T(4,128)S(1)}, u32[]{:S(2)}, u32[]{:S(2)}) %collective-permute-start.2) | collective-permute-done | bytes 2080 | tf_op jit(solution)/shard_map/ppermute | solution.py:18
  72.2 14.0 %all-gather = f32[8,12,128]{2,1,0:T(8,128)S(1)} all-gather(f32[1,12,128]{2,1,0:T(8,128)S(1)} %maximum_bitcast_fusion), channel_id=1, replica_groups=mesh['grp'=4,'dev'=8] {'dev'}, dimensions={0}, use_global_device_ids=true | all-gather | bytes 55296 | tf_op jit(solution)/shard_map/all_gather | solution.py:77
  86.2 61.1 %while.35 = (s32[]{:T(128)}, f32[4,3,128]{2,1,0:T(4,128)S(1)}, s32[4]{0:T(128)}, s32[4,64]{1,0:T(4,128)S(1)}, f32[96,5,128]{2,1,0:T(8,128)S(1)}, /*index=5*/f32[...) while((s32[]{:T(128)}, f32[4,3,128]{2,1,0:T(4,128)S(1)}, ...), condition=%wide.region_7.8_spmd.clone.clone, body=%wide.region_4.7_spmd.sunk.clone.clone.sunk | while | flops 21519628 | bytes 9044925 | solution.py:90
  90.6 1.9 %fusion.24 = f32[4,8,128,128]{3,2,1,0:T(8,128)S(1)} fusion(f32[4,8,128,128]{3,2,1,0:T(8,128)S(1)} %multiply_reduce_fusion.10, f32[4,8,128]{2,1,0:T(8,128)S(1)} %bitcast.59, f32[4,8,128]{2,1,0:T(8,128)S(1)} %get-tuple-element.869, f32[4,8,128]{2,1,0:T(8,128)S(1)} %bitcast.60, f32[4,128]{1,0:T(4,128)S(1)} %bitcast.64, ...), kind=kLoop, calls=%fused_computation.25.clone.1 | loop fusion | flops 9437184 | bytes 4265984 | tf_op jit(solution)/shard_map/while/body/eval_jaxpr/mul | solution.py:84
  92.4 1.4 multiply_reduce_fusion.11
  98.2 1.9 %fusion.24 = f32[4,8,128,128]{3,2,1,0:T(8,128)S(1)} fusion(f32[4,8,128,128]{3,2,1,0:T(8,128)S(1)} %multiply_reduce_fusion.10, f32[4,8,128]{2,1,0:T(8,128)S(1)} %bitcast.59, f32[4,8,128]{2,1,0:T(8,128)S(1)} %get-tuple-element.869, f32[4,8,128]{2,1,0:T(8,128)S(1)} %bitcast.60, f32[4,128]{1,0:T(4,128)S(1)} %bitcast.64, ...), kind=kLoop, calls=%fused_computation.25.clone.1 | loop fusion | flops 9437184 | bytes 4265984 | tf_op jit(solution)/shard_map/while/body/eval_jaxpr/mul | solution.py:84
  100.1 1.4 multiply_reduce_fusion.11
  105.9 1.9 %fusion.24 = f32[4,8,128,128]{3,2,1,0:T(8,128)S(1)} fusion(f32[4,8,128,128]{3,2,1,0:T(8,128)S(1)} %multiply_reduce_fusion.10, f32[4,8,128]{2,1,0:T(8,128)S(1)} %bitcast.59, f32[4,8,128]{2,1,0:T(8,128)S(1)} %get-tuple-element.869, f32[4,8,128]{2,1,0:T(8,128)S(1)} %bitcast.60, f32[4,128]{1,0:T(4,128)S(1)} %bitcast.64, ...), kind=kLoop, calls=%fused_computation.25.clone.1 | loop fusion | flops 9437184 | bytes 4265984 | tf_op jit(solution)/shard_map/while/body/eval_jaxpr/mul | solution.py:84
  107.7 1.4 multiply_reduce_fusion.11
  113.5 1.9 %fusion.24 = f32[4,8,128,128]{3,2,1,0:T(8,128)S(1)} fusion(f32[4,8,128,128]{3,2,1,0:T(8,128)S(1)} %multiply_reduce_fusion.10, f32[4,8,128]{2,1,0:T(8,128)S(1)} %bitcast.59, f32[4,8,128]{2,1,0:T(8,128)S(1)} %get-tuple-element.869, f32[4,8,128]{2,1,0:T(8,128)S(1)} %bitcast.60, f32[4,128]{1,0:T(4,128)S(1)} %bitcast.64, ...), kind=kLoop, calls=%fused_computation.25.clone.1 | loop fusion | flops 9437184 | bytes 4265984 | tf_op jit(solution)/shard_map/while/body/eval_jaxpr/mul | solution.py:84
  115.4 1.4 multiply_reduce_fusion.11
  121.2 1.9 %fusion.24 = f32[4,8,128,128]{3,2,1,0:T(8,128)S(1)} fusion(f32[4,8,128,128]{3,2,1,0:T(8,128)S(1)} %multiply_reduce_fusion.10, f32[4,8,128]{2,1,0:T(8,128)S(1)} %bitcast.59, f32[4,8,128]{2,1,0:T(8,128)S(1)} %get-tuple-element.869, f32[4,8,128]{2,1,0:T(8,128)S(1)} %bitcast.60, f32[4,128]{1,0:T(4,128)S(1)} %bitcast.64, ...), kind=kLoop, calls=%fused_computation.25.clone.1 | loop fusion | flops 9437184 | bytes 4265984 | tf_op jit(solution)/shard_map/while/body/eval_jaxpr/mul | solution.py:84
  123.0 1.4 multiply_reduce_fusion.11
  128.8 1.9 %fusion.24 = f32[4,8,128,128]{3,2,1,0:T(8,128)S(1)} fusion(f32[4,8,128,128]{3,2,1,0:T(8,128)S(1)} %multiply_reduce_fusion.10, f32[4,8,128]{2,1,0:T(8,128)S(1)} %bitcast.59, f32[4,8,128]{2,1,0:T(8,128)S(1)} %get-tuple-element.869, f32[4,8,128]{2,1,0:T(8,128)S(1)} %bitcast.60, f32[4,128]{1,0:T(4,128)S(1)} %bitcast.64, ...), kind=kLoop, calls=%fused_computation.25.clone.1 | loop fusion | flops 9437184 | bytes 4265984 | tf_op jit(solution)/shard_map/while/body/eval_jaxpr/mul | solution.py:84
  130.7 1.4 multiply_reduce_fusion.11
  136.4 1.9 %fusion.24 = f32[4,8,128,128]{3,2,1,0:T(8,128)S(1)} fusion(f32[4,8,128,128]{3,2,1,0:T(8,128)S(1)} %multiply_reduce_fusion.10, f32[4,8,128]{2,1,0:T(8,128)S(1)} %bitcast.59, f32[4,8,128]{2,1,0:T(8,128)S(1)} %get-tuple-element.869, f32[4,8,128]{2,1,0:T(8,128)S(1)} %bitcast.60, f32[4,128]{1,0:T(4,128)S(1)} %bitcast.64, ...), kind=kLoop, calls=%fused_computation.25.clone.1 | loop fusion | flops 9437184 | bytes 4265984 | tf_op jit(solution)/shard_map/while/body/eval_jaxpr/mul | solution.py:84
  138.3 1.4 multiply_reduce_fusion.11
  144.1 1.9 %fusion.24 = f32[4,8,128,128]{3,2,1,0:T(8,128)S(1)} fusion(f32[4,8,128,128]{3,2,1,0:T(8,128)S(1)} %multiply_reduce_fusion.10, f32[4,8,128]{2,1,0:T(8,128)S(1)} %bitcast.59, f32[4,8,128]{2,1,0:T(8,128)S(1)} %get-tuple-element.869, f32[4,8,128]{2,1,0:T(8,128)S(1)} %bitcast.60, f32[4,128]{1,0:T(4,128)S(1)} %bitcast.64, ...), kind=kLoop, calls=%fused_computation.25.clone.1 | loop fusion | flops 9437184 | bytes 4265984 | tf_op jit(solution)/shard_map/while/body/eval_jaxpr/mul | solution.py:84
  145.9 1.4 multiply_reduce_fusion.11
  (268 shorter events, 70.5 us)
Async XLA Ops:
  1.3 6.7 %collective-permute-start.1 = (f32[4,5,128]{2,1,0:T(8,128)S(1)}, f32[4,5,128]{2,1,0:T(8,128)S(1)}, u32[]{:S(2)}, u32[]{:S(2)}) collective-permute-start(f32[4,5,128]{2,1,0:T(8,128)S(1)} %copy.28), channel_id=1, source_target_pairs={{8,0},{16,8},{24,16},{0,24},{9,1},{17,9},{25,17},{1,25},{10,2},{18... | collective-permute-start | bytes 30728 | tf_op jit(solution)/shard_map/ppermute | solution.py:21
  5.3 4.6 %collective-permute-start = (f32[4,5,128]{2,1,0:T(8,128)S(1)}, f32[4,5,128]{2,1,0:T(8,128)S(1)}, u32[]{:S(2)}, u32[]{:S(2)}) collective-permute-start(f32[4,5,128]{2,1,0:T(8,128)S(1)} %copy.28), channel_id=1, source_target_pairs={{0,8},{8,16},{16,24},{24,0},{1,9},{9,17},{17,25},{25,1},{2,10},{10... | collective-permute-start | bytes 30728 | tf_op jit(solution)/shard_map/ppermute | solution.py:18
  24.6 41.9 %copy-start.1 = (f32[4,128]{1,0:T(4,128)S(1)}, f32[4,128]{1,0:T(4,128)}, u32[]{:S(2)}) copy-start(f32[4,128]{1,0:T(4,128)} %param.10) | copy-start | bytes 6148
  66.6 19.7 %copy-start = (f32[4,128]{1,0:T(4,128)}, f32[4,128]{1,0:T(4,128)S(1)}, u32[]{:S(2)}) copy-start(f32[4,128]{1,0:T(4,128)S(1)} %get-tuple-element.691) | copy-start | bytes 6148
  66.6 3.6 %collective-permute-start.3 = (f32[4,128]{1,0:T(4,128)S(1)}, f32[4,128]{1,0:T(4,128)S(1)}, u32[]{:S(2)}, u32[]{:S(2)}) collective-permute-start(f32[4,128]{1,0:T(4,128)S(1)} %multiply_divide_fusion), channel_id=1, source_target_pairs={{8,0},{16,8},{24,16},{0,24},{9,1},{17,9},{25,17},{1,25},{10,2},{18... | collective-permute-start | bytes 6152 | tf_op jit(solution)/shard_map/ppermute | solution.py:21
  67.7 4.5 %collective-permute-start.2 = (f32[4,128]{1,0:T(4,128)S(1)}, f32[4,128]{1,0:T(4,128)S(1)}, u32[]{:S(2)}, u32[]{:S(2)}) collective-permute-start(f32[4,128]{1,0:T(4,128)S(1)} %multiply_divide_fusion), channel_id=1, source_target_pairs={{0,8},{8,16},{16,24},{24,0},{1,9},{9,17},{17,25},{25,1},{2,10},{10... | collective-permute-start | bytes 6152 | tf_op jit(solution)/shard_map/ppermute | solution.py:18
where the time goes:
time: 149 us; the launch traced here: 148 us
  other arithmetic  86.7 us (58%)
  blocking collectives  28.7 us (19%)
  local copies, waits for them, and re-layouts  19.1 us (13%)
  starting transfers between devices  6 us (4%)
  waiting for transfers between devices  5.4 us (4%)
    reduce_sum x16, other arithmetic, fetch_block(): dist_sq = jnp.sum(offset * offset, axis=2)  21.1 us
    mul x8, other arithmetic, force_step(): live[:, :, None, None] * others[:, :, 3, None, :]  14.8 us
    all_gather x1, blocking collectives, on_device(): extended = lax.all_gather(rimmed, 'dev', axis=0, tiled=True)  14.7 us
    all_gather x1, blocking collectives, on_device(): weight_ext = lax.all_gather(weight_rim, 'dev', axis=0, tiled=True)  14 us
    mul x16, other arithmetic, fetch_block(): shift_blk[:, :, None, None, None] * unit_first[None, None, :, None, None]  11.7 us
    convert_element_type x16, other arithmetic, fetch_block(): ((block_at * NBLK + slot_range)[None, :] < counts[:, None]).astype(jnp.fl...  11.7 us
    reduce_sum x8, other arithmetic, density_step(): jnp.sum(live[:, :, None, None] * others[:, :, 3, None, :] * kernel, axis=...  11.5 us
    reduce_sum x8, other arithmetic, force_step(): return total - jnp.sum(factor[:, :, None] * offset, axis=(1, 4))  11.1 us
  transfers between devices with their start and end apart: 4, of which 3 were waited for; matrix products, arithmetic and copies ran while one was open for 2% of the time, Pallas kernels for 0%

commit v1 on v0

--- a/solution.py
+++ b/solution.py
@@ -7,6 +7,32 @@
 NB = 64
 NBLK = 8
 norm_const = 21.0 / (16.0 * math.pi)
+
+
+def clear_threads(load, pos_dim):
+    load = jnp.moveaxis(load, 0, pos_dim)
+    block_next = load.shape
+    return load.reshape(
+        *block_next[:pos_dim],
+        block_next[pos_dim] * block_next[pos_dim + 1],
+        *block_next[pos_dim + 2 :]
+    )
+
+
+def list_the_pools(frame_in, group_axis):
+    tall, piece_out = (lax.psum(1, group_axis), lax.axis_index(group_axis))
+    left_arr, all_rows = (frame_in[None], 1)
+    while all_rows < tall:
+        pool = []
+        for jj in range(tall):
+            pool.append((jj, jj ^ all_rows))
+        step_out = lax.ppermute(left_arr, group_axis, pool)
+        v_now = piece_out & all_rows == 0
+        left_arr = jnp.concatenate(
+            [jnp.where(v_now, left_arr, step_out), jnp.where(v_now, step_out, left_arr)]
+        )
+        all_rows *= 2
+    return left_arr
 
 
 def padded(block, sides, width):
@@ -44,7 +70,7 @@
     member_of = within // own_cells
     cell_of = within % own_cells
     rimmed = padded(particles, (("grp", 0),), own_cells)
-    extended = lax.all_gather(rimmed, "dev", axis=0, tiled=True)
+    extended = clear_threads(list_the_pools(rimmed, "dev"), 0)
     slots_ext = member_of * (3 * own_cells) + side_of * own_cells + cell_of
     upper = NB // NBLK
     slot_range = jnp.arange(NBLK, dtype=jnp.int32)

time: 149 us -> 129 us (0.87)
  other arithmetic: 86.7 us -> 67.2 us
  blocking collectives: 28.7 us -> 14 us
  waiting for transfers between devices: 5.4 us -> 15.1 us
  starting transfers between devices: 6 us -> 10.4 us
    all_gather x1 -> x0, blocking collectives: 14.7 us -> none  [on_device(): extended = lax.all_gather(rimmed, 'dev', axis=0, tiled=True)]
    mul x16, other arithmetic: 11.7 us -> 1.15 us  [fetch_block(): shift_blk[:, :, None, None, None] * unit_first[None, None, :, None, None]]
    convert_element_type x16, other arithmetic: 11.7 us -> 1.15 us  [fetch_block(): ((block_at * NBLK + slot_range)[None, :] < counts[:, None]).astype(jnp.fl...]
    ppermute x0 -> x3, waiting for transfers between devices: none -> 8.56 us  [list_the_pools(): step_out = lax.ppermute(left_arr, group_axis, pool)]
    ppermute x0 -> x3, starting transfers between devices: none -> 4.37 us  [list_the_pools(): step_out = lax.ppermute(left_arr, group_axis, pool)]
  transfers between devices with their start and end apart: 4 -> 7, of which waited for: 3 -> 7; matrix products, arithmetic and copies ran while one was open for 2% -> 3% of each run, Pallas kernels for 0% -> 0%
where the time goes in v1:
time: 129 us; the launch traced here: 128 us
  other arithmetic  67.2 us (52%)
  local copies, waits for them, and re-layouts  19.2 us (15%)
  waiting for transfers between devices  15.1 us (12%)
  blocking collectives  14 us (11%)
  starting transfers between devices  10.4 us (8%)
  loops' own time  1.39 us (1%)
    reduce_sum x16, other arithmetic, fetch_block(): dist_sq = jnp.sum(offset * offset, axis=2)  21.1 us
    mul x8, other arithmetic, force_step(): live[:, :, None, None] * others[:, :, 3, None, :]  14.8 us
    all_gather x1, blocking collectives, on_device(): weight_ext = lax.all_gather(weight_rim, 'dev', axis=0, tiled=True)  14 us
    reduce_sum x8, other arithmetic, density_step(): jnp.sum(live[:, :, None, None] * others[:, :, 3, None, :] * kernel, axis=...  11.5 us
    reduce_sum x8, other arithmetic, force_step(): return total - jnp.sum(factor[:, :, None] * offset, axis=(1, 4))  11.1 us
    gather x16, local copies, waits for them, and re-layouts, fetch_block(): others = extended[chosen]  9.35 us
    ppermute x3, waiting for transfers between devices, list_the_pools(): step_out = lax.ppermute(left_arr, group_axis, pool)  8.56 us
    gather x8, local copies, waits for them, and re-layouts, force_step(): weight_ext[chosen][:, :, None, :] * slope_j  4.59 us
  transfers between devices with their start and end apart: 7, of which 7 were waited for; matrix products, arithmetic and copies ran while one was open for 3% of the time, Pallas kernels for 0%

profile of v1, /device:TPU:0, one launch (start us, length us, event | category | flops | bytes accessed | tf_op | source)
XLA Modules:
  0.0 128.2 jit_solution(3384074377342637397)
XLA Ops:
  0.7 4.0 %collective-permute-start.1 = (f32[4,5,128]{2,0,1:T(4,128)}, f32[4,5,128]{2,0,1:T(4,128)S(1)}, u32[]{:S(2)}, u32[]{:S(2)}) collective-permute-start(f32[4,5,128]{2,0,1:T(4,128)} %param.9), channel_id=1, source_target_pairs={{8,0},{16,8},{24,16},{0,24},{9,1},{17,9},{25,17},{1,25},{10,2},{18... | collective-permute-start | bytes 30728 | tf_op jit(solution)/shard_map/ppermute | solution.py:47
  6.2 3.2 %collective-permute-done = f32[4,5,128]{2,0,1:T(4,128)S(1)} collective-permute-done((f32[4,5,128]{2,0,1:T(4,128)}, f32[4,5,128]{2,0,1:T(4,128)S(1)}, u32[]{:S(2)}, u32[]{:S(2)}) %collective-permute-start) | collective-permute-done | bytes 10272 | tf_op jit(solution)/shard_map/ppermute | solution.py:44
  12.2 1.6 %collective-permute-start.3 = (f32[2,12,5,128]{3,1,2,0:T(8,128)S(1)}, f32[2,12,5,128]{3,1,2,0:T(8,128)S(1)}, u32[]{:S(2)}, u32[]{:S(2)}) collective-permute-start(f32[2,12,5,128]{3,1,2,0:T(8,128)S(1)} %pad_maximum_fusion.2), channel_id=1, source_target_pairs={{0,2},{1,3},{2,0},{3,1},{4,6},{5,7},{6,4},{7,5},{8,10},{9,11},{10,... | collective-permute-start | bytes 184328 | tf_op jit(solution)/shard_map/ppermute | solution.py:29
  15.2 1.5 %collective-permute-done.3 = f32[2,12,5,128]{3,1,2,0:T(8,128)S(1)} collective-permute-done((f32[2,12,5,128]{3,1,2,0:T(8,128)S(1)}, f32[2,12,5,128]{3,1,2,0:T(8,128)S(1)}, u32[]{:S(2)}, u32[]{:S(2)}) %collective-permute-start.3) | collective-permute-done | bytes 61472 | tf_op jit(solution)/shard_map/ppermute | solution.py:29
  16.8 2.7 %collective-permute-start.4 = (f32[4,12,5,128]{3,1,2,0:T(8,128)S(1)}, f32[4,12,5,128]{3,1,2,0:T(8,128)S(1)}, u32[]{:S(2)}, u32[]{:S(2)}) collective-permute-start(f32[4,12,5,128]{3,1,2,0:T(8,128)S(1)} %pad_maximum_fusion.1), channel_id=1, source_target_pairs={{0,4},{1,5},{2,6},{3,7},{4,0},{5,1},{6,2},{7,3},{8,12},{9,13},{10,... | collective-permute-start | bytes 368648 | tf_op jit(solution)/shard_map/ppermute | solution.py:29
  20.1 6.5 %collective-permute-done.4 = f32[4,12,5,128]{3,1,2,0:T(8,128)S(1)} collective-permute-done((f32[4,12,5,128]{3,1,2,0:T(8,128)S(1)}, f32[4,12,5,128]{3,1,2,0:T(8,128)S(1)}, u32[]{:S(2)}, u32[]{:S(2)}) %collective-permute-start.4) | collective-permute-done | bytes 122912 | tf_op jit(solution)/shard_map/ppermute | solution.py:29
  26.9 31.4 %while.34 = (s32[]{:T(128)}, f32[4,128]{1,0:T(4,128)S(1)}, s32[4]{0:T(128)S(1)}, s32[4,64]{1,0:T(4,128)S(1)}, f32[96,5,128]{2,1,0:T(8,128)S(1)}, /*index=5*/f32[...) while((s32[]{:T(128)}, f32[4,128]{1,0:T(4,128)S(1)}, ...), condition=%wide.region_3.4_spmd.clone.clone, body=%wide.region_0.3_spmd.sunk.clone.clone.sunk | while | flops 12065039 | bytes 4628909 | solution.py:97
  29.3 1.4 %multiply_reduce_fusion.9 = f32[4,128]{1,0:T(4,128)S(1)} fusion(f32[4,8,128,128]{3,2,1,0:T(8,128)S(1)} %multiply_reduce_fusion.8, f32[4,128]{1,0:T(4,128)S(1)} %bitcast.71, f32[4,128]{1,0:T(4,128)S(1)} %divide_bitcast_fusion.6, f32[4,8,128]{2,1,0:T(8,128)S(1)} %multiply_bitcast_fusion.3), kind=kLoop, calls=%fused_computation.6.clone.1 | loop fusion | flops 6290944 | bytes 2119680 | tf_op jit(solution)/shard_map/while/body/eval_jaxpr/reduce_sum | solution.py:93
  33.3 1.4 %multiply_reduce_fusion.9 = f32[4,128]{1,0:T(4,128)S(1)} fusion(f32[4,8,128,128]{3,2,1,0:T(8,128)S(1)} %multiply_reduce_fusion.8, f32[4,128]{1,0:T(4,128)S(1)} %bitcast.71, f32[4,128]{1,0:T(4,128)S(1)} %divide_bitcast_fusion.6, f32[4,8,128]{2,1,0:T(8,128)S(1)} %multiply_bitcast_fusion.3), kind=kLoop, calls=%fused_computation.6.clone.1 | loop fusion | flops 6290944 | bytes 2119680 | tf_op jit(solution)/shard_map/while/body/eval_jaxpr/reduce_sum | solution.py:93
  37.2 1.4 %multiply_reduce_fusion.9 = f32[4,128]{1,0:T(4,128)S(1)} fusion(f32[4,8,128,128]{3,2,1,0:T(8,128)S(1)} %multiply_reduce_fusion.8, f32[4,128]{1,0:T(4,128)S(1)} %bitcast.71, f32[4,128]{1,0:T(4,128)S(1)} %divide_bitcast_fusion.6, f32[4,8,128]{2,1,0:T(8,128)S(1)} %multiply_bitcast_fusion.3), kind=kLoop, calls=%fused_computation.6.clone.1 | loop fusion | flops 6290944 | bytes 2119680 | tf_op jit(solution)/shard_map/while/body/eval_jaxpr/reduce_sum | solution.py:93
  41.1 1.4 %multiply_reduce_fusion.9 = f32[4,128]{1,0:T(4,128)S(1)} fusion(f32[4,8,128,128]{3,2,1,0:T(8,128)S(1)} %multiply_reduce_fusion.8, f32[4,128]{1,0:T(4,128)S(1)} %bitcast.71, f32[4,128]{1,0:T(4,128)S(1)} %divide_bitcast_fusion.6, f32[4,8,128]{2,1,0:T(8,128)S(1)} %multiply_bitcast_fusion.3), kind=kLoop, calls=%fused_computation.6.clone.1 | loop fusion | flops 6290944 | bytes 2119680 | tf_op jit(solution)/shard_map/while/body/eval_jaxpr/reduce_sum | solution.py:93
  45.0 1.4 %multiply_reduce_fusion.9 = f32[4,128]{1,0:T(4,128)S(1)} fusion(f32[4,8,128,128]{3,2,1,0:T(8,128)S(1)} %multiply_reduce_fusion.8, f32[4,128]{1,0:T(4,128)S(1)} %bitcast.71, f32[4,128]{1,0:T(4,128)S(1)} %divide_bitcast_fusion.6, f32[4,8,128]{2,1,0:T(8,128)S(1)} %multiply_bitcast_fusion.3), kind=kLoop, calls=%fused_computation.6.clone.1 | loop fusion | flops 6290944 | bytes 2119680 | tf_op jit(solution)/shard_map/while/body/eval_jaxpr/reduce_sum | solution.py:93
  49.0 1.4 %multiply_reduce_fusion.9 = f32[4,128]{1,0:T(4,128)S(1)} fusion(f32[4,8,128,128]{3,2,1,0:T(8,128)S(1)} %multiply_reduce_fusion.8, f32[4,128]{1,0:T(4,128)S(1)} %bitcast.71, f32[4,128]{1,0:T(4,128)S(1)} %divide_bitcast_fusion.6, f32[4,8,128]{2,1,0:T(8,128)S(1)} %multiply_bitcast_fusion.3), kind=kLoop, calls=%fused_computation.6.clone.1 | loop fusion | flops 6290944 | bytes 2119680 | tf_op jit(solution)/shard_map/while/body/eval_jaxpr/reduce_sum | solution.py:93
  52.9 1.4 %multiply_reduce_fusion.9 = f32[4,128]{1,0:T(4,128)S(1)} fusion(f32[4,8,128,128]{3,2,1,0:T(8,128)S(1)} %multiply_reduce_fusion.8, f32[4,128]{1,0:T(4,128)S(1)} %bitcast.71, f32[4,128]{1,0:T(4,128)S(1)} %divide_bitcast_fusion.6, f32[4,8,128]{2,1,0:T(8,128)S(1)} %multiply_bitcast_fusion.3), kind=kLoop, calls=%fused_computation.6.clone.1 | loop fusion | flops 6290944 | bytes 2119680 | tf_op jit(solution)/shard_map/while/body/eval_jaxpr/reduce_sum | solution.py:93
  56.8 1.4 %multiply_reduce_fusion.9 = f32[4,128]{1,0:T(4,128)S(1)} fusion(f32[4,8,128,128]{3,2,1,0:T(8,128)S(1)} %multiply_reduce_fusion.8, f32[4,128]{1,0:T(4,128)S(1)} %bitcast.71, f32[4,128]{1,0:T(4,128)S(1)} %divide_bitcast_fusion.6, f32[4,8,128]{2,1,0:T(8,128)S(1)} %multiply_bitcast_fusion.3), kind=kLoop, calls=%fused_computation.6.clone.1 | loop fusion | flops 6290944 | bytes 2119680 | tf_op jit(solution)/shard_map/while/body/eval_jaxpr/reduce_sum | solution.py:93
  58.4 2.0 %collective-permute-start.5 = (f32[4,128]{1,0:T(4,128)S(1)}, f32[4,128]{1,0:T(4,128)S(1)}, u32[]{:S(2)}, u32[]{:S(2)}) collective-permute-start(f32[4,128]{1,0:T(4,128)S(1)} %multiply_divide_fusion), channel_id=1, source_target_pairs={{0,8},{8,16},{16,24},{24,0},{1,9},{9,17},{17,25},{25,1},{2,10},{10... | collective-permute-start | bytes 6152 | tf_op jit(solution)/shard_map/ppermute | solution.py:44
  60.4 1.6 %collective-permute-done.6 = f32[4,128]{1,0:T(4,128)S(1)} collective-permute-done((f32[4,128]{1,0:T(4,128)S(1)}, f32[4,128]{1,0:T(4,128)S(1)}, u32[]{:S(2)}, u32[]{:S(2)}) %collective-permute-start.6) | collective-permute-done | bytes 2080 | tf_op jit(solution)/shard_map/ppermute | solution.py:47
  62.9 14.0 %all-gather = f32[8,12,128]{2,1,0:T(8,128)S(1)} all-gather(f32[1,12,128]{2,1,0:T(8,128)S(1)} %maximum_bitcast_fusion.1), channel_id=1, replica_groups=mesh['grp'=4,'dev'=8] {'dev'}, dimensions={0}, use_global_device_ids=true | all-gather | bytes 55296 | tf_op jit(solution)/shard_map/all_gather | solution.py:103
  76.9 50.6 %while.35 = (s32[]{:T(128)}, f32[4,3,128]{2,1,0:T(4,128)S(1)}, s32[4]{0:T(128)S(1)}, s32[4,64]{1,0:T(4,128)S(1)}, f32[96,5,128]{2,1,0:T(8,128)S(1)}, /*index=5*/...) while((s32[]{:T(128)}, f32[4,3,128]{2,1,0:T(4,128)S(1)}, ...), condition=%wide.region_7.8_spmd.clone.clone, body=%wide.region_4.7_spmd.sunk.clone.clone.sunk | while | flops 21519628 | bytes 9044925 | solution.py:116
  80.0 1.9 %fusion.24 = f32[4,8,128,128]{3,2,1,0:T(8,128)S(1)} fusion(f32[4,8,128,128]{3,2,1,0:T(8,128)S(1)} %multiply_reduce_fusion.10, f32[4,8,128]{2,1,0:T(8,128)S(1)} %bitcast.67, f32[4,8,128]{2,1,0:T(8,128)S(1)} %get-tuple-element.875, f32[4,8,128]{2,1,0:T(8,128)S(1)} %bitcast.68, f32[4,128]{1,0:T(4,128)S(1)} %bitcast.72, ...), kind=kLoop, calls=%fused_computation.25.clone.1 | loop fusion | flops 9437184 | bytes 4265984 | tf_op jit(solution)/shard_map/while/body/eval_jaxpr/mul | solution.py:110
  81.8 1.4 %multiply_reduce_fusion.11 = f32[4,3,128]{2,1,0:T(4,128)S(1)} fusion(f32[4,8,128,128]{3,2,1,0:T(8,128)S(1)} %fusion.24, f32[4,8,3]{2,1,0:T(8,128)S(1)} %broadcast_multiply_fusion.5, f32[4,8,3,128]{3,2,1,0:T(4,128)S(1)} %slice.124, f32[4,3,128]{2,1,0:T(4,128)S(1)} %slice.125), kind=kLoop, calls=%fused_computation.17.clone.1 | loop fusion | flops 6289920 | bytes 2158976 | tf_op jit(solution)/shard_map/while/body/eval_jaxpr/reduce_sum | solution.py:114
  86.3 1.9 %fusion.24 = f32[4,8,128,128]{3,2,1,0:T(8,128)S(1)} fusion(f32[4,8,128,128]{3,2,1,0:T(8,128)S(1)} %multiply_reduce_fusion.10, f32[4,8,128]{2,1,0:T(8,128)S(1)} %bitcast.67, f32[4,8,128]{2,1,0:T(8,128)S(1)} %get-tuple-element.875, f32[4,8,128]{2,1,0:T(8,128)S(1)} %bitcast.68, f32[4,128]{1,0:T(4,128)S(1)} %bitcast.72, ...), kind=kLoop, calls=%fused_computation.25.clone.1 | loop fusion | flops 9437184 | bytes 4265984 | tf_op jit(solution)/shard_map/while/body/eval_jaxpr/mul | solution.py:110
  88.2 1.4 %multiply_reduce_fusion.11 = f32[4,3,128]{2,1,0:T(4,128)S(1)} fusion(f32[4,8,128,128]{3,2,1,0:T(8,128)S(1)} %fusion.24, f32[4,8,3]{2,1,0:T(8,128)S(1)} %broadcast_multiply_fusion.5, f32[4,8,3,128]{3,2,1,0:T(4,128)S(1)} %slice.124, f32[4,3,128]{2,1,0:T(4,128)S(1)} %slice.125), kind=kLoop, calls=%fused_computation.17.clone.1 | loop fusion | flops 6289920 | bytes 2158976 | tf_op jit(solution)/shard_map/while/body/eval_jaxpr/reduce_sum | solution.py:114
  92.6 1.9 %fusion.24 = f32[4,8,128,128]{3,2,1,0:T(8,128)S(1)} fusion(f32[4,8,128,128]{3,2,1,0:T(8,128)S(1)} %multiply_reduce_fusion.10, f32[4,8,128]{2,1,0:T(8,128)S(1)} %bitcast.67, f32[4,8,128]{2,1,0:T(8,128)S(1)} %get-tuple-element.875, f32[4,8,128]{2,1,0:T(8,128)S(1)} %bitcast.68, f32[4,128]{1,0:T(4,128)S(1)} %bitcast.72, ...), kind=kLoop, calls=%fused_computation.25.clone.1 | loop fusion | flops 9437184 | bytes 4265984 | tf_op jit(solution)/shard_map/while/body/eval_jaxpr/mul | solution.py:110
  99.0 1.9 %fusion.24 = f32[4,8,128,128]{3,2,1,0:T(8,128)S(1)} fusion(f32[4,8,128,128]{3,2,1,0:T(8,128)S(1)} %multiply_reduce_fusion.10, f32[4,8,128]{2,1,0:T(8,128)S(1)} %bitcast.67, f32[4,8,128]{2,1,0:T(8,128)S(1)} %get-tuple-element.875, f32[4,8,128]{2,1,0:T(8,128)S(1)} %bitcast.68, f32[4,128]{1,0:T(4,128)S(1)} %bitcast.72, ...), kind=kLoop, calls=%fused_computation.25.clone.1 | loop fusion | flops 9437184 | bytes 4265984 | tf_op jit(solution)/shard_map/while/body/eval_jaxpr/mul | solution.py:110
  100.8 1.4 %multiply_reduce_fusion.11 = f32[4,3,128]{2,1,0:T(4,128)S(1)} fusion(f32[4,8,128,128]{3,2,1,0:T(8,128)S(1)} %fusion.24, f32[4,8,3]{2,1,0:T(8,128)S(1)} %broadcast_multiply_fusion.5, f32[4,8,3,128]{3,2,1,0:T(4,128)S(1)} %slice.124, f32[4,3,128]{2,1,0:T(4,128)S(1)} %slice.125), kind=kLoop, calls=%fused_computation.17.clone.1 | loop fusion | flops 6289920 | bytes 2158976 | tf_op jit(solution)/shard_map/while/body/eval_jaxpr/reduce_sum | solution.py:114
  105.3 1.9 %fusion.24 = f32[4,8,128,128]{3,2,1,0:T(8,128)S(1)} fusion(f32[4,8,128,128]{3,2,1,0:T(8,128)S(1)} %multiply_reduce_fusion.10, f32[4,8,128]{2,1,0:T(8,128)S(1)} %bitcast.67, f32[4,8,128]{2,1,0:T(8,128)S(1)} %get-tuple-element.875, f32[4,8,128]{2,1,0:T(8,128)S(1)} %bitcast.68, f32[4,128]{1,0:T(4,128)S(1)} %bitcast.72, ...), kind=kLoop, calls=%fused_computation.25.clone.1 | loop fusion | flops 9437184 | bytes 4265984 | tf_op jit(solution)/shard_map/while/body/eval_jaxpr/mul | solution.py:110
  107.2 1.4 %multiply_reduce_fusion.11 = f32[4,3,128]{2,1,0:T(4,128)S(1)} fusion(f32[4,8,128,128]{3,2,1,0:T(8,128)S(1)} %fusion.24, f32[4,8,3]{2,1,0:T(8,128)S(1)} %broadcast_multiply_fusion.5, f32[4,8,3,128]{3,2,1,0:T(4,128)S(1)} %slice.124, f32[4,3,128]{2,1,0:T(4,128)S(1)} %slice.125), kind=kLoop, calls=%fused_computation.17.clone.1 | loop fusion | flops 6289920 | bytes 2158976 | tf_op jit(solution)/shard_map/while/body/eval_jaxpr/reduce_sum | solution.py:114
  111.6 1.9 %fusion.24 = f32[4,8,128,128]{3,2,1,0:T(8,128)S(1)} fusion(f32[4,8,128,128]{3,2,1,0:T(8,128)S(1)} %multiply_reduce_fusion.10, f32[4,8,128]{2,1,0:T(8,128)S(1)} %bitcast.67, f32[4,8,128]{2,1,0:T(8,128)S(1)} %get-tuple-element.875, f32[4,8,128]{2,1,0:T(8,128)S(1)} %bitcast.68, f32[4,128]{1,0:T(4,128)S(1)} %bitcast.72, ...), kind=kLoop, calls=%fused_computation.25.clone.1 | loop fusion | flops 9437184 | bytes 4265984 | tf_op jit(solution)/shard_map/while/body/eval_jaxpr/mul | solution.py:110
  118.0 1.9 %fusion.24 = f32[4,8,128,128]{3,2,1,0:T(8,128)S(1)} fusion(f32[4,8,128,128]{3,2,1,0:T(8,128)S(1)} %multiply_reduce_fusion.10, f32[4,8,128]{2,1,0:T(8,128)S(1)} %bitcast.67, f32[4,8,128]{2,1,0:T(8,128)S(1)} %get-tuple-element.875, f32[4,8,128]{2,1,0:T(8,128)S(1)} %bitcast.68, f32[4,128]{1,0:T(4,128)S(1)} %bitcast.72, ...), kind=kLoop, calls=%fused_computation.25.clone.1 | loop fusion | flops 9437184 | bytes 4265984 | tf_op jit(solution)/shard_map/while/body/eval_jaxpr/mul | solution.py:110
  119.8 1.4 %multiply_reduce_fusion.11 = f32[4,3,128]{2,1,0:T(4,128)S(1)} fusion(f32[4,8,128,128]{3,2,1,0:T(8,128)S(1)} %fusion.24, f32[4,8,3]{2,1,0:T(8,128)S(1)} %broadcast_multiply_fusion.5, f32[4,8,3,128]{3,2,1,0:T(4,128)S(1)} %slice.124, f32[4,3,128]{2,1,0:T(4,128)S(1)} %slice.125), kind=kLoop, calls=%fused_computation.17.clone.1 | loop fusion | flops 6289920 | bytes 2158976 | tf_op jit(solution)/shard_map/while/body/eval_jaxpr/reduce_sum | solution.py:114
  124.3 1.9 %fusion.24 = f32[4,8,128,128]{3,2,1,0:T(8,128)S(1)} fusion(f32[4,8,128,128]{3,2,1,0:T(8,128)S(1)} %multiply_reduce_fusion.10, f32[4,8,128]{2,1,0:T(8,128)S(1)} %bitcast.67, f32[4,8,128]{2,1,0:T(8,128)S(1)} %get-tuple-element.875, f32[4,8,128]{2,1,0:T(8,128)S(1)} %bitcast.68, f32[4,128]{1,0:T(4,128)S(1)} %bitcast.72, ...), kind=kLoop, calls=%fused_computation.25.clone.1 | loop fusion | flops 9437184 | bytes 4265984 | tf_op jit(solution)/shard_map/while/body/eval_jaxpr/mul | solution.py:110
  (284 shorter events, 55.7 us)
Async XLA Ops:
  0.6 26.2 %copy-start.1 = (f32[3]{0:T(128)S(1)}, f32[3]{0:T(128)}, u32[]{:S(2)}) copy-start(f32[3]{0:T(128)} %constant.246.clone..sunk.6) | copy-start | bytes 40
  0.6 26.2 %copy-start.2 = (s32[4]{0:T(128)S(1)}, s32[4]{0:T(128)}, u32[]{:S(2)}) copy-start(s32[4]{0:T(128)} %param.12) | copy-start | bytes 52
  0.7 5.6 %collective-permute-start.1 = (f32[4,5,128]{2,0,1:T(4,128)}, f32[4,5,128]{2,0,1:T(4,128)S(1)}, u32[]{:S(2)}, u32[]{:S(2)}) collective-permute-start(f32[4,5,128]{2,0,1:T(4,128)} %param.9), channel_id=1, source_target_pairs={{8,0},{16,8},{24,16},{0,24},{9,1},{17,9},{25,17},{1,25},{10,2},{18... | collective-permute-start | bytes 30728 | tf_op jit(solution)/shard_map/ppermute | solution.py:47
  4.6 4.8 %collective-permute-start = (f32[4,5,128]{2,0,1:T(4,128)}, f32[4,5,128]{2,0,1:T(4,128)S(1)}, u32[]{:S(2)}, u32[]{:S(2)}) collective-permute-start(f32[4,5,128]{2,0,1:T(4,128)} %param.9), channel_id=1, source_target_pairs={{0,8},{8,16},{16,24},{24,0},{1,9},{9,17},{17,25},{25,1},{2,10},{10... | collective-permute-start | bytes 30728 | tf_op jit(solution)/shard_map/ppermute | solution.py:44
  10.1 1.3 %collective-permute-start.2 = (f32[1,12,5,128]{3,1,2,0:T(8,128)S(1)}, f32[1,12,5,128]{3,1,2,0:T(8,128)S(1)}, u32[]{:S(2)}, u32[]{:S(2)}) collective-permute-start(f32[1,12,5,128]{3,1,2,0:T(8,128)S(1)} %maximum_bitcast_fusion), channel_id=1, source_target_pairs={{0,1},{1,0},{2,3},{3,2},{4,5},{5,4},{6,7},{7,6},{8,9},{9,8},{10,11... | collective-permute-start | bytes 92168 | tf_op jit(solution)/shard_map/ppermute | solution.py:29
  12.2 4.6 %collective-permute-start.3 = (f32[2,12,5,128]{3,1,2,0:T(8,128)S(1)}, f32[2,12,5,128]{3,1,2,0:T(8,128)S(1)}, u32[]{:S(2)}, u32[]{:S(2)}) collective-permute-start(f32[2,12,5,128]{3,1,2,0:T(8,128)S(1)} %pad_maximum_fusion.2), channel_id=1, source_target_pairs={{0,2},{1,3},{2,0},{3,1},{4,6},{5,7},{6,4},{7,5},{8,10},{9,11},{10,... | collective-permute-start | bytes 184328 | tf_op jit(solution)/shard_map/ppermute | solution.py:29
  16.8 9.9 %collective-permute-start.4 = (f32[4,12,5,128]{3,1,2,0:T(8,128)S(1)}, f32[4,12,5,128]{3,1,2,0:T(8,128)S(1)}, u32[]{:S(2)}, u32[]{:S(2)}) collective-permute-start(f32[4,12,5,128]{3,1,2,0:T(8,128)S(1)} %pad_maximum_fusion.1), channel_id=1, source_target_pairs={{0,4},{1,5},{2,6},{3,7},{4,0},{5,1},{6,2},{7,3},{8,12},{9,13},{10,... | collective-permute-start | bytes 368648 | tf_op jit(solution)/shard_map/ppermute | solution.py:29
  26.8 31.4 %copy-start.3 = (f32[4,128]{1,0:T(4,128)S(1)}, f32[4,128]{1,0:T(4,128)}, u32[]{:S(2)}) copy-start(f32[4,128]{1,0:T(4,128)} %param.10) | copy-start | bytes 6148
  58.3 18.6 %copy-start = (f32[4,128]{1,0:T(4,128)}, f32[4,128]{1,0:T(4,128)S(1)}, u32[]{:S(2)}) copy-start(f32[4,128]{1,0:T(4,128)S(1)} %get-tuple-element.691) | copy-start | bytes 6148
  58.3 3.6 %collective-permute-start.6 = (f32[4,128]{1,0:T(4,128)S(1)}, f32[4,128]{1,0:T(4,128)S(1)}, u32[]{:S(2)}, u32[]{:S(2)}) collective-permute-start(f32[4,128]{1,0:T(4,128)S(1)} %multiply_divide_fusion), channel_id=1, source_target_pairs={{8,0},{16,8},{24,16},{0,24},{9,1},{17,9},{25,17},{1,25},{10,2},{18... | collective-permute-start | bytes 6152 | tf_op jit(solution)/shard_map/ppermute | solution.py:47
  58.4 4.5 %collective-permute-start.5 = (f32[4,128]{1,0:T(4,128)S(1)}, f32[4,128]{1,0:T(4,128)S(1)}, u32[]{:S(2)}, u32[]{:S(2)}) collective-permute-start(f32[4,128]{1,0:T(4,128)S(1)} %multiply_divide_fusion), channel_id=1, source_target_pairs={{0,8},{8,16},{16,24},{24,0},{1,9},{9,17},{17,25},{25,1},{2,10},{10... | collective-permute-start | bytes 6152 | tf_op jit(solution)/shard_map/ppermute | solution.py:44
